TPU v7x, 32 devices: a whole 2x2x4 slice. The times are simulated.
32 devices in a mesh: fsdp: 4 (over y, x), grp: 8 (over z, core).
Axes of the slice: x: 2, y: 2, z: 4, core: 2. Of those that a mesh axis runs over, the one named last changes fastest.
Arguments:
- grad_out: bfloat16 [32, 512, 512], P(('fsdp', 'grp')), may hold values from -6 to 6
- pre_first: bfloat16 [32, 512, 512], P(('fsdp', 'grp')), may hold values from -8 to 8
- pre_second: bfloat16 [32, 512, 512], P(('fsdp', 'grp')), may hold values from -8 to 8
- conv_first: bfloat16 [3, 512, 512], P(None, 'fsdp'), may hold values from -0.15625 to 0.15625
- conv_second: bfloat16 [3, 512, 512], P(None, 'fsdp'), may hold values from -0.15625 to 0.15625
- lengths: int32 [32], P(('fsdp', 'grp')), may hold values from 64 to 512
- item_ids: int32 [16384], P('grp'), may hold values from 0 to 8191
- owners: int32 [512, 1], P('grp'), may hold values from 0 to 7; in each aligned block of 64 rows (0 to 63, 64 to 127, ...) at most 16 rows name the same one
Outputs:
- table_grad: float32 [512, 65536], P('fsdp', 'grp')
Inputs may be any that keep to these rules, and one draw needn't show every extreme that they name: `owners`: among the blocks of one group, no owner is named by more than 16 blocks, a bound that some block reaches.
All inputs are finite; a program needn't handle non-finite values.
Results may differ from a plain program's by a relative error of at most 0.0037.
Values may be sent and summed in bfloat16 or wider, within the bound.
A program may use at most 64 MiB of HBM per device.

v0:
```python
import jax
import jax.numpy as jnp
from jax import lax
from jax.sharding import PartitionSpec as P

BLK = 32
ROWS_OWN = 8192


def layer_back(gradient, pre_acts, live_rows, dilation, product):
    seq_len = gradient.shape[0]
    pre_float = pre_acts.astype(jnp.float32)
    sig_val = jax.nn.sigmoid(pre_float)
    deltas = (gradient * sig_val * (1.0 + pre_float * (1.0 - sig_val))).astype(jnp.bfloat16)
    padded = jnp.pad(deltas, ((dilation, dilation), (0, 0)))
    tap_rows = jnp.stack(
        [
            padded[2 * dilation : 2 * dilation + seq_len],
            padded[dilation : dilation + seq_len],
            padded[0:seq_len],
        ]
    )
    return gradient + live_rows * product(tap_rows)


def gathered_product(weights):

    def apply_taps(tap_rows):
        return jnp.einsum(
            "ktd,kpd->tp",
            tap_rows,
            lax.all_gather(weights, "fsdp", axis=1, tiled=True),
            preferred_element_type=jnp.float32,
        )

    return apply_taps


def body(grad_out, pre_first, pre_second, conv_first, conv_second, lengths, item_ids, owners):
    seq_len = grad_out.shape[1]
    positions = jnp.arange(seq_len, dtype=jnp.int32)
    live_rows = (positions < lengths[0]).astype(jnp.float32)[:, None]
    gradient = grad_out[0].astype(jnp.float32)
    gradient = layer_back(gradient, pre_second[0], live_rows, 2, gathered_product(conv_second))
    gradient = layer_back(gradient, pre_first[0], live_rows, 1, gathered_product(conv_first))
    row_grad = (live_rows * gradient).astype(jnp.bfloat16)
    group_cols = lax.all_to_all(row_grad.T, "fsdp", split_axis=0, concat_axis=1, tiled=True)
    feat_cols = group_cols.shape[0]
    owner_count = lax.axis_size("grp")
    blocks = owners.shape[0]
    slot_cap = max(2, 2 * blocks // owner_count)
    block_dest = owners[:, 0]
    dest_hits = (block_dest[:, None] == jnp.arange(owner_count, dtype=jnp.int32)[None, :]).astype(
        jnp.int32
    )
    earlier = jnp.cumsum(dest_hits, axis=0) - dest_hits
    block_rank = jnp.sum(dest_hits * earlier, axis=1)
    slot_index = block_dest * slot_cap + block_rank
    select_int = (
        slot_index[:, None] == jnp.arange(owner_count * slot_cap, dtype=jnp.int32)[None, :]
    ).astype(jnp.int32)
    select_int = select_int.reshape(blocks, owner_count, slot_cap)
    select_map = select_int.astype(jnp.bfloat16)
    block_cols = group_cols.reshape(feat_cols, blocks, BLK)
    send_rows = jnp.einsum(
        "cbr,bos->ocsr", block_cols, select_map, preferred_element_type=jnp.float32
    )
    send_rows = send_rows.astype(jnp.bfloat16).reshape(owner_count, feat_cols, slot_cap * BLK)
    shifted_ids = item_ids.reshape(blocks, BLK) + 1
    send_ids = jnp.einsum("br,bos->osr", shifted_ids, select_int) - 1
    send_ids = send_ids.reshape(owner_count, slot_cap * BLK)
    recv_rows, recv_ids = (
        lax.all_to_all(send_rows, "grp", split_axis=0, concat_axis=0, tiled=True),
        lax.all_to_all(send_ids, "grp", split_axis=0, concat_axis=0, tiled=True),
    )
    flat_rows = jnp.transpose(recv_rows, (0, 2, 1)).reshape(-1, feat_cols).astype(jnp.float32)
    safe_ids = jnp.where(recv_ids < 0, ROWS_OWN, recv_ids).reshape(-1)
    summed = jax.ops.segment_sum(flat_rows, safe_ids, num_segments=ROWS_OWN + 1)
    return summed[:ROWS_OWN].T


def solution(mesh):
    placed = (
        P(("fsdp", "grp"), None, None),
        P(("fsdp", "grp"), None, None),
        P(("fsdp", "grp"), None, None),
        P(None, "fsdp", None),
        P(None, "fsdp", None),
        P(("fsdp", "grp")),
        P("grp"),
        P("grp", None),
    )
    return jax.shard_map(
        body, mesh=mesh, in_specs=placed, out_specs=P("fsdp", "grp"), check_vma=False
    )
```

profile of v0, /device:TPU:0, one launch (start us, length us, event | category | flops | bytes accessed | tf_op | source)
XLA Modules:
  0.0 175.9 jit_solution(7663716986740653124)
XLA Ops:
  6.5 0.0 all-gather.3.cloned.1.call-start
  6.5 0.7 all-gather.3.cloned.1.call-update
  7.3 0.0 all-gather.5.cloned.1.call-start
  7.3 0.7 all-gather.5.cloned.1.call-update
  8.7 0.7 fusion.74
  9.4 0.1 reduce_window_sum.11
  9.5 0.8 select_reduce_fusion
  10.3 0.0 copy-start.2
  10.3 0.0 copy-start
  10.3 0.0 copy-start.1
  10.4 1.7 fusion.46
  12.1 0.0 copy-start.4
  12.1 0.2 slice_bitcast_fusion.4
  12.3 0.0 copy-done.2
  12.3 0.0 copy-done
  12.3 0.0 copy-done.1
  12.4 0.5 fusion.48
  12.8 30.0 %all-gather.3.cloned.1.call-done = bf16[3,512,512]{2,1,0:T(8,128)(2,1)} async-done(((bf16[3,128,512]{2,1,0:T(8,128)(2,1)}), bf16[3,512,512]{2,1,0:T(8,128)(2,1)}) %all-gather.3.cloned.1.call-update) | async-done | bytes 1572880 | tf_op jit(solution)/shard_map/all_gather | solution.py:32
  42.8 0.0 copy-done.4
  42.8 3.7 %fusion.54 = (bf16[512,512]{1,0:T(8,128)(2,1)S(1)}, f32[512,512]{1,0:T(8,128)}) fusion(bf16[1,512,512]{2,1,0:T(8,128)(2,1)S(1)} %copy-done.4, bf16[3,512,512]{2,1,0:T(8,128)(2,1)} %all-gather.3.cloned.1.call-done, bf16[1,512,512]{2,1,0:T(8,128)(2,1)S(1)} %get-tuple-element.8, bf16[1,512,512]{2,1,0:T(8,128)(2,1)S(1)} %fusion.48, ...), kind=kOutput, calls=%fused_computation.47 | convolution fusion | flops 810287104 | bytes 5769216 | tf_op jit(solution)/shard_map/ktd,kpd->tp/dot_general | solution.py:29
  46.4 0.0 copy-start.5
  46.4 0.2 slice_bitcast_fusion.2
  46.7 28.8 %all-gather.5.cloned.1.call-done = bf16[3,512,512]{2,1,0:T(8,128)(2,1)} async-done(((bf16[3,128,512]{2,1,0:T(8,128)(2,1)}), bf16[3,512,512]{2,1,0:T(8,128)(2,1)}) %all-gather.5.cloned.1.call-update) | async-done | bytes 1572880 | tf_op jit(solution)/shard_map/all_gather | solution.py:32
  75.5 0.0 copy-done.5
  75.5 2.4 %fusion.42 = bf16[64,4,8,128]{3,2,1,0:T(8,128)(2,1)S(1)} fusion(f32[512,512]{1,0:T(8,128)S(1)} %copy-done.5, bf16[3,512,512]{2,1,0:T(8,128)(2,1)} %all-gather.5.cloned.1.call-done, bf16[1,512,512]{2,1,0:T(8,128)(2,1)S(1)} %get-tuple-element.6, bf16[1,512,512]{2,1,0:T(8,128)(2,1)S(1)} %bitcast.101, bf16[1,512,512]{2,1,0:T(8,128)(2,1)S(1)} %get-tuple-element.5, ...), kind=kOutput, calls=%fused_computation.36 | convolution fusion | flops 807927808 | bytes 4720640 | tf_op jit(solution)/shard_map/ktd,kpd->tp/dot_general | solution.py:29
  77.9 0.0 copy-start.3
  77.9 0.9 copy.34
  78.8 3.5 %all-to-all-start.1 = ((bf16[4,128,512]{1,2,0:T(8,128)(2,1)}), bf16[4,128,512]{1,2,0:T(8,128)(2,1)S(1)}, u32[]{:S(2)}, u32[]{:S(2)}) async-start(bf16[4,128,512]{1,2,0:T(8,128)(2,1)} %bitcast.97), calls=%async_computation.1 | async-start | bytes 1048576 | tf_op jit(solution)/shard_map/all_to_all | solution.py:47
  82.3 0.0 copy-done.3
  82.3 0.1 add.52
  82.4 0.2 convolution_add_fusion
  82.6 0.7 all_to_all.30
  83.3 7.1 %all-to-all-done.1 = bf16[4,128,512]{1,2,0:T(8,128)(2,1)S(1)} async-done(((bf16[4,128,512]{1,2,0:T(8,128)(2,1)}), bf16[4,128,512]{1,2,0:T(8,128)(2,1)S(1)}, u32[]{:S(2)}, u32[]{:S(2)}) %all-to-all-start.1) | async-done | bytes 524320 | tf_op jit(solution)/shard_map/all_to_all | solution.py:47
  90.4 4.6 %all-to-all-start = ((s32[8,1,512]{2,1,0:T(1,128)}), s32[8,1,512]{2,1,0:T(1,128)S(1)}, u32[]{:S(2)}, u32[]{:S(2)}) async-start(s32[8,1,512]{2,1,0:T(1,128)} %all_to_all.30), calls=%async_computation | async-start | bytes 32768 | tf_op jit(solution)/shard_map/all_to_all | solution.py:74
  95.0 0.5 fusion.14
  95.5 1.2 copy.21
  96.7 3.9 %all-to-all-done = s32[8,1,512]{2,1,0:T(1,128)S(1)} async-done(((s32[8,1,512]{2,1,0:T(1,128)}), s32[8,1,512]{2,1,0:T(1,128)S(1)}, u32[]{:S(2)}, u32[]{:S(2)}) %all-to-all-start) | async-done | bytes 16416 | tf_op jit(solution)/shard_map/all_to_all | solution.py:74
  100.7 3.6 %all-to-all-start.2 = ((bf16[8,128,512]{1,2,0:T(8,128)(2,1)}), bf16[8,128,512]{1,2,0:T(8,128)(2,1)S(1)}, u32[]{:S(2)}, u32[]{:S(2)}) async-start(bf16[8,128,512]{1,2,0:T(8,128)(2,1)} %bitcast.25), calls=%async_computation.2 | async-start | bytes 2097152 | tf_op jit(solution)/shard_map/all_to_all | solution.py:73
  104.2 26.5 %all-to-all-done.2 = bf16[8,128,512]{1,2,0:T(8,128)(2,1)S(1)} async-done(((bf16[8,128,512]{1,2,0:T(8,128)(2,1)}), bf16[8,128,512]{1,2,0:T(8,128)(2,1)S(1)}, u32[]{:S(2)}, u32[]{:S(2)}) %all-to-all-start.2) | async-done | bytes 1048608 | tf_op jit(solution)/shard_map/all_to_all | solution.py:73
  130.7 0.1 convert_element_type.105
  130.9 28.2 %scatter_custom_fusion = f32[8193,128]{1,0:T(8,128)} fusion(s32[4096]{0:T(1024)S(1)} %bitcast.103, f32[4096,128]{1,0:T(8,128)S(1)} %bitcast.99, f32[]{:T(128)} %constant.8.clone.1), kind=kCustom, calls=%fused_computation.2 | custom fusion | flops 524288 | bytes 4194820 | tf_op jit(solution)/shard_map/scatter-add | solution.py:78
  159.1 4.4 %slice_bitcast_fusion = f32[128,8192]{0,1:T(8,128)} fusion(f32[8193,128]{1,0:T(8,128)} %scatter_custom_fusion), kind=kLoop, calls=%fused_computation.1 | loop fusion | bytes 8388608 | tf_op jit(solution)/shard_map/transpose | solution.py:79
  163.5 5.6 %copy.22 = f32[128,8192]{1,0:T(8,128)} copy(f32[128,8192]{0,1:T(8,128)} %slice_bitcast_fusion) | data formatting | bytes 8388608 | tf_op jit(solution)/shard_map/transpose | solution.py:79
  (5 shorter events, 0.0 us)
Async XLA Ops:
  6.5 36.2 %all-gather.3.cloned.1.call-start = ((), (), s32[]{:S(2)}) async-start(), calls=%async_computation.3 | async-start | bytes 1966080 | tf_op jit(solution)/shard_map/all_gather | solution.py:32
  7.3 68.2 %all-gather.5.cloned.1.call-start = ((), (), s32[]{:S(2)}) async-start(), calls=%async_computation.4 | async-start | bytes 1966080 | tf_op jit(solution)/shard_map/all_gather | solution.py:32
  10.3 2.0 %copy-start.2 = (s32[2048]{0:T(1024)S(1)}, s32[2048]{0:T(1024)}, u32[]{:S(2)}) copy-start(s32[2048]{0:T(1024)} %param.14) | copy-start | bytes 24580
  10.3 2.0 %copy-start = (bf16[1,512,512]{2,1,0:T(8,128)(2,1)S(1)}, bf16[1,512,512]{2,1,0:T(8,128)(2,1)}, u32[]{:S(2)}) copy-start(bf16[1,512,512]{2,1,0:T(8,128)(2,1)} %param.10) | copy-start | bytes 1572868
  10.3 2.0 %copy-start.1 = (bf16[1,512,512]{2,1,0:T(8,128)(2,1)S(1)}, bf16[1,512,512]{2,1,0:T(8,128)(2,1)}, u32[]{:S(2)}) copy-start(bf16[1,512,512]{2,1,0:T(8,128)(2,1)} %param.8) | copy-start | bytes 1572868
  12.1 30.7 %copy-start.4 = (bf16[1,512,512]{2,1,0:T(8,128)(2,1)S(1)}, bf16[1,512,512]{2,1,0:T(8,128)(2,1)}, u32[]{:S(2)}) copy-start(bf16[1,512,512]{2,1,0:T(8,128)(2,1)} %param.9) | copy-start | bytes 1572868
  46.4 29.0 %copy-start.5 = (f32[512,512]{1,0:T(8,128)S(1)}, f32[512,512]{1,0:T(8,128)}, u32[]{:S(2)}) copy-start(f32[512,512]{1,0:T(8,128)} %get-tuple-element.10) | copy-start | bytes 3145732
  77.9 4.4 %copy-start.3 = (s32[64,1]{0,1:T(1,128)S(1)}, s32[64,1]{0,1:T(1,128)}, u32[]{:S(2)}) copy-start(s32[64,1]{0,1:T(1,128)} %param.15) | copy-start | bytes 772
  78.8 11.6 %all-to-all-start.1 = ((bf16[4,128,512]{1,2,0:T(8,128)(2,1)}), bf16[4,128,512]{1,2,0:T(8,128)(2,1)S(1)}, u32[]{:S(2)}, u32[]{:S(2)}) async-start(bf16[4,128,512]{1,2,0:T(8,128)(2,1)} %bitcast.97), calls=%async_computation.1 | async-start | bytes 1048576 | tf_op jit(solution)/shard_map/all_to_all | solution.py:47
  90.4 10.3 %all-to-all-start = ((s32[8,1,512]{2,1,0:T(1,128)}), s32[8,1,512]{2,1,0:T(1,128)S(1)}, u32[]{:S(2)}, u32[]{:S(2)}) async-start(s32[8,1,512]{2,1,0:T(1,128)} %all_to_all.30), calls=%async_computation | async-start | bytes 32768 | tf_op jit(solution)/shard_map/all_to_all | solution.py:74
  100.7 30.1 %all-to-all-start.2 = ((bf16[8,128,512]{1,2,0:T(8,128)(2,1)}), bf16[8,128,512]{1,2,0:T(8,128)(2,1)S(1)}, u32[]{:S(2)}, u32[]{:S(2)}) async-start(bf16[8,128,512]{1,2,0:T(8,128)(2,1)} %bitcast.25), calls=%async_computation.2 | async-start | bytes 2097152 | tf_op jit(solution)/shard_map/all_to_all | solution.py:73
Sparse Core Ops, SparseCore 0:
  9.2 33.5 all-gather.2
  44.6 30.8 all-gather.4
where the time goes:
time: 176 us
  waiting for transfers between devices  97.7 us (56%)
  other arithmetic  32.2 us (18%)
  between operations  14.2 us (8%)
  local copies, waits for them, and re-layouts  13.4 us (8%)
  starting transfers between devices  11.7 us (7%)
  matrix products  6.8 us (4%)
    all_gather x2, waiting for transfers between devices, apply_taps(): lax.all_gather(weights, 'fsdp', axis=1, tiled=True)  58.8 us
    scatter-add x1, other arithmetic, body(): summed = jax.ops.segment_sum(flat_rows, safe_ids, num_segments=ROWS_OWN + 1)  28.2 us
    all_to_all x1, waiting for transfers between devices, body(): lax.all_to_all(send_rows, 'grp', split_axis=0, concat_axis=0, tiled=True)  26.5 us
    transpose x2, local copies, waits for them, and re-layouts, body(): return summed[:ROWS_OWN].T  10 us
    all_to_all x1, waiting for transfers between devices, body(): lax.all_to_all(row_grad.T, 'fsdp', split_axis=0, concat_axis=1, tiled=True)  7.07 us
    dot_general x2, matrix products, apply_taps(): jnp.einsum('ktd,kpd->tp', tap_rows, lax.all_gather(weights, 'fsdp', axis=...  6.08 us
    all_to_all x1, starting transfers between devices, body(): lax.all_to_all(send_ids, 'grp', split_axis=0, concat_axis=0, tiled=True)  4.6 us
    all_to_all x1, waiting for transfers between devices, body(): lax.all_to_all(send_ids, 'grp', split_axis=0, concat_axis=0, tiled=True)  3.93 us
  transfers between devices with their start and end apart: 5, of which 5 were waited for; matrix products, arithmetic and copies ran while one was open for 6% of the time, Pallas kernels for 0%

commit v1 on v0

--- a/solution.py
+++ b/solution.py
@@ -5,6 +5,28 @@
 
 BLK = 32
 ROWS_OWN = 8192
+
+
+def joined_along(blocks, dim):
+    blocks = jnp.moveaxis(blocks, 0, dim)
+    shape = blocks.shape
+    return blocks.reshape(*shape[:dim], shape[dim] * shape[dim + 1], *shape[dim + 2 :])
+
+
+def ring_gather(array, axis, dim):
+    peers = lax.axis_size(axis)
+    pairs = [(i, (i + 1) % peers) for i in range(peers)]
+    back = [(b, a) for a, b in pairs]
+    lower, upper = ([], [])
+    for step in range(peers - 1):
+        if step % 2 == 0:
+            lower.append(lax.ppermute(lower[-1] if lower else array, axis, pairs))
+        else:
+            upper.append(lax.ppermute(upper[-1] if upper else array, axis, back))
+    parts = jnp.stack([*lower[::-1], array, *upper])
+    shift = lax.axis_index(axis) - len(lower)
+    parts = parts[(jnp.arange(peers) - shift) % peers]
+    return joined_along(parts, dim)
 
 
 def layer_back(gradient, pre_acts, live_rows, dilation, product):
@@ -29,7 +51,7 @@
         return jnp.einsum(
             "ktd,kpd->tp",
             tap_rows,
-            lax.all_gather(weights, "fsdp", axis=1, tiled=True),
+            ring_gather(weights, "fsdp", 1),
             preferred_element_type=jnp.float32,
         )
 

time: 176 us -> 154 us (0.88)
  waiting for transfers between devices: 97.7 us -> 74.2 us
  between operations: 14.2 us -> 0.9 us
  starting transfers between devices: 11.7 us -> 20.8 us
  local copies, waits for them, and re-layouts: 13.4 us -> 19.8 us
  matrix products: 6.8 us -> 3.03 us
  other arithmetic: 32.2 us -> 35.2 us
    all_gather x2 -> x0, waiting for transfers between devices: 58.8 us -> none  [apply_taps(): lax.all_gather(weights, 'fsdp', axis=1, tiled=True)]
    ppermute x0 -> x6, waiting for transfers between devices: none -> 37.1 us  [the longest x4 37.1 us: ring_gather(): lower.append(lax.ppermute(lower[-1] if lower else array, axis, pairs))]
    ppermute x0 -> x6, starting transfers between devices: none -> 8.98 us  [the longest x4 6.17 us: ring_gather(): lower.append(lax.ppermute(lower[-1] if lower else array, axis, pairs))]
    dot_general x2, matrix products: 6.08 us -> 2.32 us  [apply_taps(): jnp.einsum('ktd,kpd->tp', tap_rows, ring_gather(weights, 'fsdp', 1), pref...]
    unnamed x12 -> x26, local copies, waits for them, and re-layouts: 0.04 us -> 2.68 us
  transfers between devices with their start and end apart: 5 -> 9, of which waited for: 5 -> 7; matrix products, arithmetic and copies ran while one was open for 6% -> 7% of each run, Pallas kernels for 0% -> 0%
where the time goes in v1:
time: 154 us
  waiting for transfers between devices  74.2 us (48%)
  other arithmetic  35.2 us (23%)
  starting transfers between devices  20.8 us (14%)
  local copies, waits for them, and re-layouts  19.8 us (13%)
  matrix products  3.03 us (2%)
    ppermute x4, waiting for transfers between devices, ring_gather(): lower.append(lax.ppermute(lower[-1] if lower else array, axis, pairs))  37.1 us
    scatter-add x1, other arithmetic, body(): summed = jax.ops.segment_sum(flat_rows, safe_ids, num_segments=ROWS_OWN + 1)  28.2 us
    all_to_all x1, waiting for transfers between devices, body(): lax.all_to_all(send_rows, 'grp', split_axis=0, concat_axis=0, tiled=True)  26.5 us
    transpose x2, local copies, waits for them, and re-layouts, body(): return summed[:ROWS_OWN].T  10 us
    all_to_all x1, waiting for transfers between devices, body(): lax.all_to_all(row_grad.T, 'fsdp', split_axis=0, concat_axis=1, tiled=True)  6.65 us
    ppermute x4, starting transfers between devices, ring_gather(): lower.append(lax.ppermute(lower[-1] if lower else array, axis, pairs))  6.17 us
    all_to_all x1, starting transfers between devices, body(): lax.all_to_all(send_ids, 'grp', split_axis=0, concat_axis=0, tiled=True)  4.78 us
    all_to_all x1, waiting for transfers between devices, body(): lax.all_to_all(send_ids, 'grp', split_axis=0, concat_axis=0, tiled=True)  3.93 us
  transfers between devices with their start and end apart: 9, of which 7 were waited for; matrix products, arithmetic and copies ran while one was open for 7% of the time, Pallas kernels for 0%

profile of v1, /device:TPU:0, one launch (start us, length us, event | category | flops | bytes accessed | tf_op | source)
XLA Modules:
  0.0 153.9 jit_solution(12950307782741568837)
XLA Ops:
  0.0 3.0 %collective-permute-start.3 = (bf16[3,128,512]{2,1,0:T(8,128)(2,1)}, bf16[3,128,512]{2,1,0:T(8,128)(2,1)S(1)}, u32[]{:S(2)}, u32[]{:S(2)}) collective-permute-start(bf16[3,128,512]{2,1,0:T(8,128)(2,1)} %param.11), channel_id=1, source_target_pairs={{0,8},{8,16},{16,24},{24,0},{1,9},{9,17},{17,25},{25,1},{2,10},{10... | collective-permute-start | bytes 1179656 | tf_op jit(solution)/shard_map/ppermute | solution.py:23
  3.0 1.0 collective-permute-start.5
  3.9 1.1 collective-permute-start
  5.0 1.9 %collective-permute-start.2 = (bf16[3,128,512]{2,1,0:T(8,128)(2,1)}, bf16[3,128,512]{2,1,0:T(8,128)(2,1)}, u32[]{:S(2)}, u32[]{:S(2)}) collective-permute-start(bf16[3,128,512]{2,1,0:T(8,128)(2,1)} %param.12), channel_id=1, source_target_pairs={{8,0},{16,8},{24,16},{0,24},{9,1},{17,9},{25,17},{1,25},{10,2},{18... | collective-permute-start | bytes 1179656 | tf_op jit(solution)/shard_map/ppermute | solution.py:25
  7.5 0.7 fusion.74
  8.2 0.1 reduce_window_sum.11
  8.3 1.4 select_reduce_fusion
  9.8 1.7 %fusion.46 = bf16[512,512]{1,0:T(8,128)(2,1)S(1)} fusion(bf16[1,512,512]{2,1,0:T(8,128)(2,1)} %param.8, bf16[1,512,512]{2,1,0:T(8,128)(2,1)} %param.10), kind=kLoop, calls=%fused_computation.43 | loop fusion | flops 2883584 | bytes 1572864 | tf_op jit(solution)/shard_map/convert_element_type | solution.py:36
  11.5 0.0 copy-start.9
  11.5 0.0 copy-start.7
  11.5 1.2 slice_bitcast_fusion.4
  12.7 0.0 copy-done
  12.7 0.0 copy-done.1
  12.7 1.3 fusion.48
  14.0 0.1 collective-permute-done.3
  14.1 1.1 collective-permute-start.4
  15.2 15.8 %collective-permute-done = bf16[3,128,512]{2,1,0:T(8,128)(2,1)S(1)} collective-permute-done((bf16[3,128,512]{2,1,0:T(8,128)(2,1)}, bf16[3,128,512]{2,1,0:T(8,128)(2,1)S(1)}, u32[]{:S(2)}, u32[]{:S(2)}) %collective-permute-start) | collective-permute-done | bytes 393248 | tf_op jit(solution)/shard_map/ppermute | solution.py:23
  30.9 1.1 collective-permute-start.1
  32.0 0.0 copy-done.9
  32.0 0.0 collective-permute-done.5
  32.0 15.8 %collective-permute-done.4 = bf16[3,128,512]{2,1,0:T(8,128)(2,1)S(1)} collective-permute-done((bf16[3,128,512]{2,1,0:T(8,128)(2,1)S(1)}, bf16[3,128,512]{2,1,0:T(8,128)(2,1)S(1)}, u32[]{:S(2)}, u32[]{:S(2)}) %collective-permute-start.4) | collective-permute-done | bytes 393248 | tf_op jit(solution)/shard_map/ppermute | solution.py:23
  47.8 0.0 copy-done.7
  47.8 0.2 pad_maximum_fusion.1
  48.0 0.6 gather_fusion.1
  48.7 0.0 copy-start.8
  48.7 1.3 copy.27
  50.0 0.0 collective-permute-done.2
  50.0 5.5 %collective-permute-done.1 = bf16[3,128,512]{2,1,0:T(8,128)(2,1)} collective-permute-done((bf16[3,128,512]{2,1,0:T(8,128)(2,1)S(1)}, bf16[3,128,512]{2,1,0:T(8,128)(2,1)}, u32[]{:S(2)}, u32[]{:S(2)}) %collective-permute-start.1) | collective-permute-done | bytes 393248 | tf_op jit(solution)/shard_map/ppermute | solution.py:23
  55.5 0.0 copy-done.8
  55.5 1.3 pad_maximum_fusion
  56.8 0.6 gather_fusion
  57.5 0.0 copy-start.2
  57.5 0.0 copy-start.4
  57.5 0.0 copy-start.5
  57.5 0.0 copy-start.12
  57.5 0.2 copy.26
  57.7 0.8 copy-done.2
  58.5 0.2 copy-done.4
  58.7 0.2 copy-done.5
  58.8 0.2 copy-done.6
  59.0 0.2 copy-done.12
  59.1 1.3 fusion.54
  60.4 0.0 copy-start.3
  60.5 0.2 slice_bitcast_fusion.2
  60.7 1.2 copy-done.3
  61.9 1.0 fusion.42
  62.9 0.0 copy-start.10
  62.9 0.0 copy-start.11
  62.9 0.9 copy.44
  63.8 3.5 %all-to-all-start.1 = ((bf16[4,128,512]{1,2,0:T(8,128)(2,1)}), bf16[4,128,512]{1,2,0:T(8,128)(2,1)S(1)}, u32[]{:S(2)}, u32[]{:S(2)}) async-start(bf16[4,128,512]{1,2,0:T(8,128)(2,1)} %bitcast.111), calls=%async_computation.1 | async-start | bytes 1048576 | tf_op jit(solution)/shard_map/all_to_all | solution.py:69
  67.3 0.1 add.79
  67.4 0.2 convolution_add_fusion
  67.6 0.7 all_to_all.30
  68.3 6.6 %all-to-all-done.1 = bf16[4,128,512]{1,2,0:T(8,128)(2,1)S(1)} async-done(((bf16[4,128,512]{1,2,0:T(8,128)(2,1)}), bf16[4,128,512]{1,2,0:T(8,128)(2,1)S(1)}, u32[]{:S(2)}, u32[]{:S(2)}) %all-to-all-start.1) | async-done | bytes 524320 | tf_op jit(solution)/shard_map/all_to_all | solution.py:69
  75.0 4.8 %all-to-all-start = ((s32[8,1,512]{2,1,0:T(1,128)}), s32[8,1,512]{2,1,0:T(1,128)S(1)}, u32[]{:S(2)}, u32[]{:S(2)}) async-start(s32[8,1,512]{2,1,0:T(1,128)} %all_to_all.30), calls=%async_computation | async-start | bytes 32768 | tf_op jit(solution)/shard_map/all_to_all | solution.py:96
  79.8 0.5 fusion.14
  80.2 1.2 copy.31
  81.5 3.9 %all-to-all-done = s32[8,1,512]{2,1,0:T(1,128)S(1)} async-done(((s32[8,1,512]{2,1,0:T(1,128)}), s32[8,1,512]{2,1,0:T(1,128)S(1)}, u32[]{:S(2)}, u32[]{:S(2)}) %all-to-all-start) | async-done | bytes 16416 | tf_op jit(solution)/shard_map/all_to_all | solution.py:96
  85.4 3.6 %all-to-all-start.2 = ((bf16[8,128,512]{1,2,0:T(8,128)(2,1)}), bf16[8,128,512]{1,2,0:T(8,128)(2,1)S(1)}, u32[]{:S(2)}, u32[]{:S(2)}) async-start(bf16[8,128,512]{1,2,0:T(8,128)(2,1)} %bitcast.38), calls=%async_computation.2 | async-start | bytes 2097152 | tf_op jit(solution)/shard_map/all_to_all | solution.py:95
  89.0 26.5 %all-to-all-done.2 = bf16[8,128,512]{1,2,0:T(8,128)(2,1)S(1)} async-done(((bf16[8,128,512]{1,2,0:T(8,128)(2,1)}), bf16[8,128,512]{1,2,0:T(8,128)(2,1)S(1)}, u32[]{:S(2)}, u32[]{:S(2)}) %all-to-all-start.2) | async-done | bytes 1048608 | tf_op jit(solution)/shard_map/all_to_all | solution.py:95
  115.5 0.1 convert_element_type.105
  115.6 28.2 %scatter_custom_fusion = f32[8193,128]{1,0:T(8,128)} fusion(s32[4096]{0:T(1024)S(1)} %bitcast.127, f32[4096,128]{1,0:T(8,128)S(1)} %bitcast.115, f32[]{:T(128)} %constant.39.clone.1), kind=kCustom, calls=%fused_computation.4 | custom fusion | flops 524288 | bytes 4194820 | tf_op jit(solution)/shard_map/scatter-add | solution.py:100
  143.8 4.4 %slice_bitcast_fusion = f32[128,8192]{0,1:T(8,128)} fusion(f32[8193,128]{1,0:T(8,128)} %scatter_custom_fusion), kind=kLoop, calls=%fused_computation.3 | loop fusion | bytes 8388608 | tf_op jit(solution)/shard_map/transpose | solution.py:101
  148.3 5.6 %copy.32 = f32[128,8192]{1,0:T(8,128)} copy(f32[128,8192]{0,1:T(8,128)} %slice_bitcast_fusion) | data formatting | bytes 8388608 | tf_op jit(solution)/shard_map/transpose | solution.py:101
  (12 shorter events, 0.1 us)
Async XLA Ops:
  0.0 14.1 %collective-permute-start.3 = (bf16[3,128,512]{2,1,0:T(8,128)(2,1)}, bf16[3,128,512]{2,1,0:T(8,128)(2,1)S(1)}, u32[]{:S(2)}, u32[]{:S(2)}) collective-permute-start(bf16[3,128,512]{2,1,0:T(8,128)(2,1)} %param.11), channel_id=1, source_target_pairs={{0,8},{8,16},{16,24},{24,0},{1,9},{9,17},{17,25},{25,1},{2,10},{10... | collective-permute-start | bytes 1179656 | tf_op jit(solution)/shard_map/ppermute | solution.py:23
  3.0 29.1 %collective-permute-start.5 = (bf16[3,128,512]{2,1,0:T(8,128)(2,1)}, bf16[3,128,512]{2,1,0:T(8,128)(2,1)S(1)}, u32[]{:S(2)}, u32[]{:S(2)}) collective-permute-start(bf16[3,128,512]{2,1,0:T(8,128)(2,1)} %param.11), channel_id=1, source_target_pairs={{8,0},{16,8},{24,16},{0,24},{9,1},{17,9},{25,17},{1,25},{10,2},{18... | collective-permute-start | bytes 1179656 | tf_op jit(solution)/shard_map/ppermute | solution.py:25
  3.9 27.0 %collective-permute-start = (bf16[3,128,512]{2,1,0:T(8,128)(2,1)}, bf16[3,128,512]{2,1,0:T(8,128)(2,1)S(1)}, u32[]{:S(2)}, u32[]{:S(2)}) collective-permute-start(bf16[3,128,512]{2,1,0:T(8,128)(2,1)} %param.12), channel_id=1, source_target_pairs={{0,8},{8,16},{16,24},{24,0},{1,9},{9,17},{17,25},{25,1},{2,10},{10... | collective-permute-start | bytes 1179656 | tf_op jit(solution)/shard_map/ppermute | solution.py:23
  5.0 45.0 %collective-permute-start.2 = (bf16[3,128,512]{2,1,0:T(8,128)(2,1)}, bf16[3,128,512]{2,1,0:T(8,128)(2,1)}, u32[]{:S(2)}, u32[]{:S(2)}) collective-permute-start(bf16[3,128,512]{2,1,0:T(8,128)(2,1)} %param.12), channel_id=1, source_target_pairs={{8,0},{16,8},{24,16},{0,24},{9,1},{17,9},{25,17},{1,25},{10,2},{18... | collective-permute-start | bytes 1179656 | tf_op jit(solution)/shard_map/ppermute | solution.py:25
  9.8 3.0 %copy-start = (bf16[1,512,512]{2,1,0:T(8,128)(2,1)S(1)}, bf16[1,512,512]{2,1,0:T(8,128)(2,1)}, u32[]{:S(2)}) copy-start(bf16[1,512,512]{2,1,0:T(8,128)(2,1)} %param.10) | copy-start | bytes 1572868
  9.8 3.0 %copy-start.1 = (bf16[1,512,512]{2,1,0:T(8,128)(2,1)S(1)}, bf16[1,512,512]{2,1,0:T(8,128)(2,1)}, u32[]{:S(2)}) copy-start(bf16[1,512,512]{2,1,0:T(8,128)(2,1)} %param.8) | copy-start | bytes 1572868
  11.5 20.5 %copy-start.9 = (s32[2048]{0:T(1024)S(1)}, s32[2048]{0:T(1024)}, u32[]{:S(2)}) copy-start(s32[2048]{0:T(1024)} %param.14) | copy-start | bytes 24580
  11.5 36.3 %copy-start.7 = (bf16[3,128,512]{2,1,0:T(8,128)(2,1)S(1)}, bf16[3,128,512]{2,1,0:T(8,128)(2,1)}, u32[]{:S(2)}) copy-start(bf16[3,128,512]{2,1,0:T(8,128)(2,1)} %param.11) | copy-start | bytes 1179652
  14.1 33.7 %collective-permute-start.4 = (bf16[3,128,512]{2,1,0:T(8,128)(2,1)S(1)}, bf16[3,128,512]{2,1,0:T(8,128)(2,1)S(1)}, u32[]{:S(2)}, u32[]{:S(2)}) collective-permute-start(bf16[3,128,512]{2,1,0:T(8,128)(2,1)S(1)} %collective-permute-done.3), channel_id=1, source_target_pairs={{0,8},{8,16},{16,24},{24,0},{1,9},{9,17},{17,25},{25,1},{2,10},{10... | collective-permute-start | bytes 1179656 | tf_op jit(solution)/shard_map/ppermute | solution.py:23
  30.9 24.5 %collective-permute-start.1 = (bf16[3,128,512]{2,1,0:T(8,128)(2,1)S(1)}, bf16[3,128,512]{2,1,0:T(8,128)(2,1)}, u32[]{:S(2)}, u32[]{:S(2)}) collective-permute-start(bf16[3,128,512]{2,1,0:T(8,128)(2,1)S(1)} %collective-permute-done), channel_id=1, source_target_pairs={{0,8},{8,16},{16,24},{24,0},{1,9},{9,17},{17,25},{25,1},{2,10},{10... | collective-permute-start | bytes 1179656 | tf_op jit(solution)/shard_map/ppermute | solution.py:23
  48.7 6.8 %copy-start.8 = (bf16[3,128,512]{2,1,0:T(8,128)(2,1)S(1)}, bf16[3,128,512]{2,1,0:T(8,128)(2,1)}, u32[]{:S(2)}) copy-start(bf16[3,128,512]{2,1,0:T(8,128)(2,1)} %param.12) | copy-start | bytes 1179652
  57.5 1.0 copy-start.2
  57.5 1.2 copy-start.4
  57.5 1.3 copy-start.5
  57.5 1.5 copy-start.6
  57.5 1.6 %copy-start.12 = (bf16[1,512,512]{2,1,0:T(8,128)(2,1)S(1)}, bf16[1,512,512]{2,1,0:T(8,128)(2,1)}, u32[]{:S(2)}) copy-start(bf16[1,512,512]{2,1,0:T(8,128)(2,1)} %param.9) | copy-start | bytes 1572868
  60.4 1.4 copy-start.3
  62.9 4.4 %copy-start.10 = (s32[64,1]{0,1:T(1,128)S(1)}, s32[64,1]{0,1:T(1,128)}, u32[]{:S(2)}) copy-start(s32[64,1]{0,1:T(1,128)} %param.15) | copy-start | bytes 772
  62.9 4.4 %copy-start.11 = (s32[64]{0:T(128)S(1)}, s32[64]{0:T(128)}, u32[]{:S(2)}) copy-start(s32[64]{0:T(128)} %select_reduce_fusion) | copy-start | bytes 772
  63.8 11.2 %all-to-all-start.1 = ((bf16[4,128,512]{1,2,0:T(8,128)(2,1)}), bf16[4,128,512]{1,2,0:T(8,128)(2,1)S(1)}, u32[]{:S(2)}, u32[]{:S(2)}) async-start(bf16[4,128,512]{1,2,0:T(8,128)(2,1)} %bitcast.111), calls=%async_computation.1 | async-start | bytes 1048576 | tf_op jit(solution)/shard_map/all_to_all | solution.py:69
  75.0 10.4 %all-to-all-start = ((s32[8,1,512]{2,1,0:T(1,128)}), s32[8,1,512]{2,1,0:T(1,128)S(1)}, u32[]{:S(2)}, u32[]{:S(2)}) async-start(s32[8,1,512]{2,1,0:T(1,128)} %all_to_all.30), calls=%async_computation | async-start | bytes 32768 | tf_op jit(solution)/shard_map/all_to_all | solution.py:96
  85.4 30.1 %all-to-all-start.2 = ((bf16[8,128,512]{1,2,0:T(8,128)(2,1)}), bf16[8,128,512]{1,2,0:T(8,128)(2,1)S(1)}, u32[]{:S(2)}, u32[]{:S(2)}) async-start(bf16[8,128,512]{1,2,0:T(8,128)(2,1)} %bitcast.38), calls=%async_computation.2 | async-start | bytes 2097152 | tf_op jit(solution)/shard_map/all_to_all | solution.py:95
